TPU v7x, 256 devices: a whole 4x4x8 slice. The times are simulated.
256 devices in a mesh: rows: 128 (over x, y_hi, z, core), cols: 2 (over y_lo).
Axes of the slice: x: 4, y: 4 (y_hi: 2, y_lo: 2; y = y_hi * 2 + y_lo), z: 8, core: 2. Of those that a mesh axis runs over, the one named last changes fastest.
Arguments:
- ancestor: bfloat16 [24576, 24576], P('rows', 'cols'), may hold values from -6 to 6
- panel_below: bfloat16 [2048, 512], P('rows'), may hold values from -0.0625 to 0.0625
- panel_beside: bfloat16 [2048, 512], P('rows'), may hold values from -0.0625 to 0.0625
- inverse_lower: bfloat16 [512, 512], replicated, may hold values from -3 to 3
- inverse_upper: bfloat16 [512, 512], replicated, may hold values from -3 to 3
- list_below: int32 [16], replicated, may hold values from 0 to 191, as said below
- list_beside: int32 [16], replicated, may hold values from 0 to 191, as said below
- second_below: bfloat16 [2048, 512], P('rows'), may hold values from -0.0625 to 0.0625
- second_beside: bfloat16 [2048, 512], P('rows'), may hold values from -0.0625 to 0.0625
- linked_below: bfloat16 [512, 512], replicated, may hold values from -0.0625 to 0.0625
- linked_beside: bfloat16 [512, 512], replicated, may hold values from -0.0625 to 0.0625
- second_lower: bfloat16 [512, 512], replicated, may hold values from -3 to 3
- second_upper: bfloat16 [512, 512], replicated, may hold values from -3 to 3
- blocks_below: int32 [16], replicated, may hold values from 0 to 191, as said below
- blocks_beside: int32 [16], replicated, may hold values from 0 to 191, as said below
Outputs:
- new_lower: bfloat16 [24576, 512], P('rows', 'cols')
- new_upper: bfloat16 [24576, 512], P(('cols', 'rows'))
- new_diagonal: bfloat16 [512, 512], P(None, 'cols')
- next_lower: bfloat16 [24576, 512], P('rows', 'cols')
- next_upper: bfloat16 [24576, 512], P(('cols', 'rows'))
- next_link: bfloat16 [512, 512], replicated
- next_diagonal: bfloat16 [512, 512], P(None, 'cols')
Inputs may be any that keep to these rules, and one draw needn't show every extreme that they name: `list_below`: 16 distinct block numbers in ascending order; block 0 and block 191 are always listed. `list_beside`: 16 distinct block numbers in ascending order; block 0 and block 191 are always listed. `blocks_below`: 16 distinct block numbers in ascending order; block 0 and block 191 are always listed. `blocks_beside`: 16 distinct block numbers in ascending order; block 0 and block 191 are always listed.
All inputs are finite; a program needn't handle non-finite values.
Results may differ from a plain program's by a relative error of at most 0.0077.
Values may be sent and summed in bfloat16 or wider, within the bound.
A program may use at most 128 MiB of HBM per device.

v0:
```python
import jax
import jax.numpy as jnp
from jax import lax
from jax.sharding import PartitionSpec as P

BLK = 128


def normalise(panel, inverse):
    return jnp.dot(panel, inverse, preferred_element_type=jnp.float32).astype(jnp.bfloat16)


def normalise_by_rows(panel, inverse):
    return lax.dot_general(
        panel, inverse, (((1,), (1,)), ((), ())), preferred_element_type=jnp.float32
    ).astype(jnp.bfloat16)


def inner_rows(left, right):
    return lax.dot_general(
        left, right, (((0,), (0,)), ((), ())), preferred_element_type=jnp.float32
    )


def own_half(panel, first_column, half_width):
    return lax.dynamic_slice_in_dim(panel, first_column, half_width, 1)


def listed_columns(tile, blocks, first_block):
    block_count = tile.shape[1] // BLK
    local_ids = blocks - first_block
    inside = jnp.logical_and(local_ids >= 0, local_ids < block_count)
    picked = jnp.take(
        tile.reshape(tile.shape[0], block_count, BLK),
        jnp.clip(local_ids, 0, block_count - 1),
        axis=1,
    )
    return (picked.reshape(tile.shape[0], blocks.shape[0] * BLK), jnp.repeat(inside, BLK))


def masked_product(picked, inside, panel):
    kept = jnp.where(inside[:, None], panel, jnp.zeros_like(panel))
    return jnp.dot(picked, kept, preferred_element_type=jnp.float32)


def listed_rows(strips, blocks):
    shaped = strips.reshape(strips.shape[0] // BLK, BLK, strips.shape[1])
    return jnp.take(shaped, blocks, axis=0).reshape(blocks.shape[0] * BLK, strips.shape[1])


def rows_onto(panel, blocks, first_row, row_count):
    global_rows = first_row + jnp.arange(row_count, dtype=jnp.int32)
    block_of = global_rows // BLK
    offset = global_rows % BLK
    matches = block_of[:, None] == blocks[None, :]
    position = jnp.sum(
        jnp.where(matches, jnp.arange(blocks.shape[0], dtype=jnp.int32)[None, :], 0), axis=1
    )
    present = jnp.any(matches, axis=1)
    picked = jnp.take(panel, position * BLK + offset, axis=0)
    return jnp.where(present[:, None], picked, jnp.zeros_like(picked))


def lower_block(partial_value):
    return (-lax.psum_scatter(partial_value, "cols", scatter_dimension=1, tiled=True)).astype(
        jnp.bfloat16
    )


def diag_block(base_value, picked_rows, lower_local):
    summed = lax.psum(inner_rows(picked_rows, lower_local), "rows")
    return (base_value - summed).astype(jnp.bfloat16)


def body(
    ancestor,
    panel_below,
    panel_beside,
    inverse_lower,
    inverse_upper,
    list_below,
    list_beside,
    second_below,
    second_beside,
    linked_below,
    linked_beside,
    second_lower,
    second_upper,
    blocks_below,
    blocks_beside,
):
    row_devices = lax.axis_size("rows")
    row_at = lax.axis_index("rows")
    col_at = lax.axis_index("cols")
    col_devices = lax.axis_size("cols")
    tile_rows = ancestor.shape[0]
    tile_cols = ancestor.shape[1]
    width = inverse_lower.shape[0]
    half_width = width // col_devices
    first_column = col_at * half_width
    unit_below = normalise(panel_below, inverse_lower)
    unit_beside = normalise_by_rows(panel_beside, inverse_upper)
    below_next = normalise(second_below, second_lower)
    beside_next = normalise_by_rows(second_beside, second_upper)
    unit_below, unit_beside, below_next, beside_next = (
        lax.all_gather(unit_below, "rows", axis=0, tiled=True),
        lax.all_gather(unit_beside, "rows", axis=0, tiled=True),
        lax.all_gather(below_next, "rows", axis=0, tiled=True),
        lax.all_gather(beside_next, "rows", axis=0, tiled=True),
    )
    strips = lax.all_to_all(ancestor, "rows", split_axis=1, concat_axis=0, tiled=True)
    strip_width = tile_cols // row_devices
    strip_start = (col_at * row_devices + row_at) * strip_width
    first_block = col_at * (tile_cols // BLK)
    row_start = row_at * tile_rows
    picked, inside = listed_columns(ancestor, list_below, first_block)
    new_lower = lower_block(masked_product(picked, inside, unit_below))
    new_upper = (-inner_rows(listed_rows(strips, list_beside), unit_beside)).astype(jnp.bfloat16)
    base_first = jnp.dot(
        inverse_upper,
        own_half(inverse_lower, first_column, half_width),
        preferred_element_type=jnp.float32,
    )
    new_diagonal = diag_block(
        base_first, rows_onto(unit_beside, list_beside, row_start, tile_rows), new_lower
    )
    link_below = normalise(linked_below, second_lower)
    link_beside = normalise_by_rows(linked_beside, second_upper)
    link_rows = lax.dynamic_slice_in_dim(link_below, first_column, half_width, 0)
    picked_next, inside_next = listed_columns(ancestor, blocks_below, first_block)
    partial_value = masked_product(picked_next, inside_next, below_next) + jnp.dot(
        new_lower, link_rows, preferred_element_type=jnp.float32
    )
    next_lower = lower_block(partial_value)
    first_row = (row_at == 0).astype(jnp.float32)
    link_term = inner_rows(
        new_upper, rows_onto(below_next, blocks_below, strip_start, strip_width)
    ) + first_row * jnp.dot(new_diagonal, link_rows, preferred_element_type=jnp.float32)
    next_link = (-lax.psum(link_term, ("rows", "cols"))).astype(jnp.bfloat16)
    next_upper = (
        -(
            inner_rows(listed_rows(strips, blocks_beside), beside_next)
            + jnp.dot(new_upper, link_beside, preferred_element_type=jnp.float32)
        )
    ).astype(jnp.bfloat16)
    base_second = jnp.dot(
        second_upper,
        own_half(second_lower, first_column, half_width),
        preferred_element_type=jnp.float32,
    ) - inner_rows(link_beside, own_half(next_link, first_column, half_width))
    next_diagonal = diag_block(
        base_second, rows_onto(beside_next, blocks_beside, row_start, tile_rows), next_lower
    )
    return (new_lower, new_upper, new_diagonal, next_lower, next_upper, next_link, next_diagonal)


def solution(mesh):
    return jax.shard_map(
        body,
        mesh=mesh,
        in_specs=(
            P("rows", "cols"),
            P("rows", None),
            P("rows", None),
            P(),
            P(),
            P(),
            P(),
            P("rows", None),
            P("rows", None),
            P(),
            P(),
            P(),
            P(),
            P(),
            P(),
        ),
        out_specs=(
            P("rows", "cols"),
            P(("cols", "rows"), None),
            P(None, "cols"),
            P("rows", "cols"),
            P(("cols", "rows"), None),
            P(),
            P(None, "cols"),
        ),
        check_vma=False,
    )
```

profile of v0, /device:TPU:153, one launch (start us, length us, event | category | flops | bytes accessed | tf_op | source)
XLA Modules:
  0.0 2097.3 jit_solution(3499471611282957993)
XLA Ops:
  7.2 0.0 all-gather.5.cloned.1.call-start
  7.2 1.9 convolution_convert_fusion.4
  9.2 0.0 all-gather.9.cloned.1.call-start
  9.2 1.5 convolution_convert_fusion.2
  10.7 0.0 reduce-scatter.3.cloned.1.call-start
  10.8 0.7 compare_and_fusion.2
  11.5 5.8 copy_bitcast_fusion
  17.3 3.0 gather_fusion.1
  20.3 0.1 broadcast_bitcast_fusion.1
  20.4 105.6 %all-gather.5.cloned.1.call-done = bf16[2048,512]{1,0:T(8,128)(2,1)} async-done(((bf16[16,512]{1,0:T(8,128)(2,1)}), bf16[2048,512]{1,0:T(8,128)(2,1)}) %all-gather.5.cloned.1.call-update) | async-done | bytes 2097168 | tf_op jit(solution)/shard_map/all_gather | solution.py:106
  126.0 3.1 fusion.2
  129.1 0.0 all-gather.11.cloned.1.call-start
  129.1 0.9 convolution_convert_fusion.1
  130.0 10.1 all_to_all.12
  140.1 9.4 copy.76
  149.5 13.6 all-to-all-start
  163.2 0.0 all-gather.7.cloned.1.call-start
  163.3 0.9 convolution_convert_fusion.3
  164.1 0.0 reduce-scatter.5.cloned.1.call-start
  164.2 3.0 gather_fusion.4
  167.3 0.1 fusion.46
  167.5 0.1 fusion.47
  167.6 0.1 broadcast_bitcast_fusion
  167.7 0.4 fusion.66
  168.1 83.6 %all-gather.9.cloned.1.call-done = bf16[2048,512]{1,0:T(8,128)(2,1)} async-done(((bf16[16,512]{1,0:T(8,128)(2,1)}), bf16[2048,512]{1,0:T(8,128)(2,1)}) %all-gather.9.cloned.1.call-update) | async-done | bytes 2097168 | tf_op jit(solution)/shard_map/all_gather | solution.py:108
  251.7 2.2 fusion
  254.0 21.3 %reduce-scatter.3.cloned.1.call-done = f32[192,256]{1,0:T(8,128)} async-done(((f32[192,512]{1,0:T(8,128)}), f32[192,256]{1,0:T(8,128)}) %reduce-scatter.3.cloned.1.call-update) | async-done | bytes 196624 | tf_op jit(solution)/shard_map/reduce_scatter | solution.py:65
  275.3 0.9 negate_convert_fusion.2
  276.3 1.0 convolution_add_fusion.1
  277.3 0.2 all-reduce.6.cloned.1.call-start
  277.5 0.1 compare_reduce_fusion.2
  277.6 0.1 compare_reduce_fusion
  277.7 119.4 %all-gather.11.cloned.1.call-done = bf16[2048,512]{1,0:T(8,128)(2,1)} async-done(((bf16[16,512]{1,0:T(8,128)(2,1)}), bf16[2048,512]{1,0:T(8,128)(2,1)}) %all-gather.11.cloned.1.call-update) | async-done | bytes 2097168 | tf_op jit(solution)/shard_map/all_gather | solution.py:109
  397.1 2.9 gather_fusion.6
  400.0 114.1 %all-gather.7.cloned.1.call-done = bf16[2048,512]{1,0:T(8,128)(2,1)} async-done(((bf16[16,512]{1,0:T(8,128)(2,1)}), bf16[2048,512]{1,0:T(8,128)(2,1)}) %all-gather.7.cloned.1.call-update) | async-done | bytes 2097168 | tf_op jit(solution)/shard_map/all_gather | solution.py:107
  514.1 2.9 gather_fusion.3
  517.1 1.1 fusion.30
  518.2 16.2 reduce-scatter.5.cloned.1.call-done
  534.4 0.9 negate_convert_fusion.1
  535.3 0.6 copy-done.14
  536.0 1.1 fusion.29
  537.1 0.0 all-reduce.4.cloned.1.call-start
  537.2 0.5 compare_and_fusion.6
  537.8 0.5 compare_and_fusion.4
  538.3 1.5 convolution_convert_fusion
  539.8 3.3 gather_fusion
  543.1 1204.2 %all-reduce.6.cloned.1.call-done = (f32[512,256]{0,1:T(8,128)}, f32[512,256]{0,1:T(8,128)}) async-done(((f32[512,256]{0,1:T(8,128)}, f32[512,256]{0,1:T(8,128)}), (f32[512,256]{0,1:T(8,128)}, f32[512,256]{0,1:T(8,128)})) %all-reduce.6.cloned.1.call-update) | async-done | bytes 1048592 | tf_op jit(solution)/shard_map/psum | solution.py:71
  1747.3 1.4 fusion.10
  1748.6 0.8 copy.87
  1749.5 1.3 convolution_multiply_fusion
  1750.8 8.2 copy.78
  1759.0 3.0 gather_fusion.2
  1762.0 1.3 fusion.12
  1763.3 0.6 copy-done.11
  1763.9 1.3 convolution_add_fusion
  1765.3 3.0 gather_fusion.5
  1768.3 0.5 fusion.20
  1768.8 0.4 copy-done.12
  1769.2 0.9 fusion.13
  1770.0 316.4 %all-reduce.4.cloned.1.call-done = f32[512,512]{1,0:T(8,128)} async-done(((f32[512,512]{1,0:T(8,128)}), f32[512,512]{1,0:T(8,128)}) %all-reduce.4.cloned.1.call-update) | async-done | bytes 1048592 | tf_op jit(solution)/shard_map/psum | solution.py:139
  2086.5 1.3 negate_convert_fusion
  2087.8 0.3 fusion.25
  2088.2 1.4 fusion.9
  2089.6 0.8 copy.88
  (62 shorter events, 0.4 us)
Async XLA Ops:
  7.2 2.0 copy-start
  7.2 118.8 %all-gather.5.cloned.1.call-start = ((), (), s32[]{:S(2)}) async-start(), calls=%async_computation.3 | async-start | bytes 2113536 | tf_op jit(solution)/shard_map/all_gather | solution.py:106
  9.2 242.6 %all-gather.9.cloned.1.call-start = ((), (), s32[]{:S(2)}) async-start(), calls=%async_computation.6 | async-start | bytes 2113536 | tf_op jit(solution)/shard_map/all_gather | solution.py:108
  10.7 264.6 %reduce-scatter.3.cloned.1.call-start = ((), (), s32[]{:S(2)}) async-start(), calls=%async_computation.4 | async-start | bytes 589824 | tf_op jit(solution)/shard_map/reduce_scatter | solution.py:65
  126.0 3.1 copy-start.2
  126.0 3.1 copy-start.15
  129.1 268.1 %all-gather.11.cloned.1.call-start = ((), (), s32[]{:S(2)}) async-start(), calls=%async_computation.8 | async-start | bytes 2113536 | tf_op jit(solution)/shard_map/all_gather | solution.py:109
  149.5 13.7 copy-start.5
  149.5 13.7 copy-start.16
  149.5 1601.3 %all-to-all-start = ((bf16[192,128,96]{2,0,1:T(8,128)(2,1)}), bf16[192,128,96]{2,0,1:T(8,128)(2,1)}, u32[]{:S(2)}, u32[]{:S(2)}) async-start(bf16[192,128,96]{2,0,1:T(8,128)(2,1)} %copy.76), calls=%async_computation.1 | async-start | bytes 12582912 | tf_op jit(solution)/shard_map/all_to_all | solution.py:111
  163.1 4.2 copy-start.17
  163.2 4.2 copy-start.18
  163.2 4.3 copy-start.19
  163.2 4.5 copy-start.10
  163.2 350.9 %all-gather.7.cloned.1.call-start = ((), (), s32[]{:S(2)}) async-start(), calls=%async_computation.5 | async-start | bytes 2113536 | tf_op jit(solution)/shard_map/all_gather | solution.py:107
  164.1 370.2 %reduce-scatter.5.cloned.1.call-start = ((), (), s32[]{:S(2)}) async-start(), calls=%async_computation.7 | async-start | bytes 589824 | tf_op jit(solution)/shard_map/reduce_scatter | solution.py:65
  276.3 240.8 %copy-start.9 = (bf16[192,256]{1,0:T(8,128)(2,1)}, bf16[192,256]{1,0:T(8,128)(2,1)S(1)}, u32[]{:S(2)}) copy-start(bf16[192,256]{1,0:T(8,128)(2,1)S(1)} %negate_convert_fusion.2) | copy-start | bytes 294916
  277.3 1469.9 %all-reduce.6.cloned.1.call-start = ((), (), s32[]{:S(2)}) async-start(), calls=%async_computation.10 | async-start | bytes 2097152 | tf_op jit(solution)/shard_map/psum | solution.py:71
  535.3 0.6 copy-start.14
  536.0 1211.3 %copy-start.8 = (bf16[512,512]{1,0:T(8,128)(2,1)S(1)}, bf16[512,512]{1,0:T(8,128)(2,1)}, u32[]{:S(2)}) copy-start(bf16[512,512]{1,0:T(8,128)(2,1)} %param.24) | copy-start | bytes 1572868
  537.1 1549.3 %all-reduce.4.cloned.1.call-start = ((), (), s32[]{:S(2)}) async-start(), calls=%async_computation.9 | async-start | bytes 2097152 | tf_op jit(solution)/shard_map/psum | solution.py:139
  1750.8 11.2 copy-start.7
  1762.0 1.9 copy-start.4
  1762.0 1.9 copy-start.13
  1762.0 1.9 copy-start.20
  1763.3 0.6 copy-start.11
  1763.9 4.3 copy-start.1
  1768.3 0.9 copy-start.12
  1769.2 319.0 %copy-start.3 = (bf16[512,512]{1,0:T(8,128)(2,1)S(1)}, bf16[512,512]{1,0:T(8,128)(2,1)}, u32[]{:S(2)}) copy-start(bf16[512,512]{1,0:T(8,128)(2,1)} %param.33) | copy-start | bytes 1572868
  2087.8 2.6 copy-start.6
Sparse Core Ops, SparseCore 0:
  12.3 113.6 all-gather.4
  130.3 121.3 all-gather.8
  254.8 20.4 reduce-scatter.2
  279.5 117.6 all-gather.10
  401.3 112.8 all-gather.6
  516.5 17.8 reduce-scatter.4
  537.6 1209.6 all-reduce.5
  1765.4 321.0 all-reduce.3
where the time goes:
time: 2100 us
  waiting for transfers between devices  1980 us (94%)
  local copies, waits for them, and re-layouts  58.1 us (3%)
  matrix products  24.1 us (1%)
    psum x1, waiting for transfers between devices, diag_block(): summed = lax.psum(inner_rows(picked_rows, lower_local), 'rows')  1200 us
    psum x1, waiting for transfers between devices, body(): next_link = (-lax.psum(link_term, ('rows', 'cols'))).astype(jnp.bfloat16)  316 us
    all_gather x1, waiting for transfers between devices, body(): lax.all_gather(beside_next, 'rows', axis=0, tiled=True)  119 us
    all_gather x1, waiting for transfers between devices, body(): lax.all_gather(unit_beside, 'rows', axis=0, tiled=True)  114 us
    all_gather x1, waiting for transfers between devices, body(): lax.all_gather(unit_below, 'rows', axis=0, tiled=True)  106 us
    all_gather x1, waiting for transfers between devices, body(): lax.all_gather(below_next, 'rows', axis=0, tiled=True)  83.6 us
  transfers between devices with their start and end apart: 9, of which 8 were waited for; matrix products, arithmetic and copies ran while one was open for 3% of the time, Pallas kernels for 0%

commit v1 on v0

v1 whole, which is shorter than its diff:
```python
import jax
import jax.numpy as jnp
from jax import lax
from jax.experimental import pallas as pl
from jax.experimental.pallas import tpu as pltpu
from jax.sharding import PartitionSpec as P

MESH = pl.DeviceIdType.MESH
F32 = jnp.float32
BF16 = jnp.bfloat16
NX, NY, NZ, NK = 4, 2, 8, 2
NXY = NX * NY
NQ = NXY * NK
ND = NQ * 2
BLK = 128
W = 512
HALF = 256
R = 16
ROWS = 192
COLS = 12288
STRIP = COLS // NQ
OWN = 96


def dot(a, b):
    return jnp.dot(a, b, preferred_element_type=F32)


def dot_rows(a, b):
    return lax.dot_general(a, b, (((0,), (0,)), ((), ())), preferred_element_type=F32)


def dot_cols(a, b):
    return lax.dot_general(a, b, (((1,), (1,)), ((), ())), preferred_element_type=F32)


def kept(block, keep):
    scale = jnp.full((1, block.shape[1]), keep.astype(jnp.int32).astype(F32), F32).astype(BF16)
    return block * scale


def each(n, body):
    def step(i, carry):
        body(i)
        return carry

    lax.fori_loop(0, n, step, 0)


def kernel(
    anc, p_below, p_beside, inv_l, inv_u, s_below, s_beside, lk_below, lk_beside, sec_l, sec_u,
    list_below, list_beside, blocks_below, blocks_beside,
    o_lower, o_upper, o_diag, o_nlower, o_nupper, o_link, o_ndiag,
    tile, strip, unit, pick_l, pick_u, onto, prod, low_s, low_r, sums_s, sums_r, zsum, fin, up_s, up_r,
    link_b, link_s, base1, base2,
    loc_sem, gy_s, gy_r, gx_s, gx_r, zr_s, zr_r, zl_s, zl_r, gc_s, gc_r,
    aa_s, aa_r, lw_s, lw_r, sm_s, sm_r, zs_s, zs_r, fn_s, fn_r, up_ss, up_rs,
):
    row = lax.axis_index("rows")
    col = lax.axis_index("cols")
    core = lax.rem(row, NK)
    z = lax.rem(lax.div(row, NK), NZ)
    xy = lax.div(row, NK * NZ)
    x = lax.div(xy, NY)
    yh = lax.rem(xy, NY)
    q = xy * NK + core
    d = q * 2 + col

    def row_of(xy_, z_, core_):
        return (xy_ * NZ + z_) * NK + core_

    def copy(src, dst, s, r, to_row, to_col):
        return pltpu.make_async_remote_copy(
            src_ref=src, dst_ref=dst, send_sem=s, recv_sem=r,
            device_id=(to_row, to_col), device_id_type=MESH,
        )

    def strip_cols(q_):
        return pl.ds(pl.multiple_of(q_ * STRIP, BLK), STRIP)

    own_half = pl.ds(pl.multiple_of(col * HALF, BLK), HALF)
    other_half = pl.ds(pl.multiple_of((1 - col) * HALF, BLK), HALF)

    def load_block(j):
        pltpu.make_async_copy(
            anc.at[:, :, pl.ds(pl.multiple_of(j * BLK, BLK), BLK)], tile.at[j], loc_sem.at[0]
        ).start()

    each(COLS // BLK, load_block)
    load_strip = pltpu.make_async_copy(
        anc.at[:, :, strip_cols(q)], strip.at[pl.ds(q * 3, 3)], loc_sem.at[1]
    )
    load_strip.start()

    unit[0, xy, z, core] = dot(p_below[...], inv_l[...]).astype(BF16)
    unit[1, xy, z, core] = dot(s_below[...], sec_l[...]).astype(BF16)
    unit[2, xy, z, core] = dot_cols(p_beside[...], inv_u[...]).astype(BF16)
    unit[3, xy, z, core] = dot_cols(s_beside[...], sec_u[...]).astype(BF16)

    barrier = pltpu.get_barrier_semaphore()

    def greet_plane(i):
        peer = lax.rem(d + 1 + i, ND)
        pq = lax.div(peer, 2)
        pl.semaphore_signal(
            barrier, inc=1,
            device_id=(row_of(lax.div(pq, NK), z, lax.rem(pq, NK)), lax.rem(peer, 2)),
            device_id_type=MESH,
        )

    def greet_line(i):
        peer = lax.rem(z + 1 + lax.div(i, NK), NZ)
        pl.semaphore_signal(
            barrier, inc=1, device_id=(row_of(xy, peer, lax.rem(i, NK)), col), device_id_type=MESH
        )

    each(ND - 1, greet_plane)
    each((NZ - 1) * NK, greet_line)
    pl.semaphore_wait(barrier, ND - 1 + (NZ - 1) * NK)

    nxy = x * NY + (1 - yh)
    mine = unit.at[:, xy, z, core]
    y_out = copy(mine, mine, gy_s.at[0], gy_r.at[0], row_of(nxy, z, core), 1 - col)
    y_out.start()
    theirs = unit.at[:, nxy, z, core]
    copy(theirs, theirs, gy_s.at[0], gy_r.at[0], row_of(nxy, z, core), 1 - col).wait_recv()

    def x_copy(i, holder, to):
        part = unit.at[:, pl.ds(holder * NY, NY), z, core]
        return copy(part, part, gx_s.at[i - 1], gx_r.at[i - 1], row_of(to * NY + yh, z, core), col)

    for i in (1, 3, 2):
        x_copy(i, x, lax.rem(x + i, NX)).start()

    def aa_copy(i, src_q, to_q):
        return copy(
            anc.at[:, :, strip_cols(to_q)],
            strip.at[pl.ds(src_q * 3, 3)],
            aa_s.at[i], aa_r.at[i],
            row_of(lax.div(to_q, NK), z, lax.rem(to_q, NK)), col,
        )

    each(NQ - 1, lambda i: aa_copy(i, q, lax.rem(q + 1 + i, NQ)).start())

    for i in (1, 3, 2):
        frm = lax.rem(x + NX - i, NX)
        x_copy(i, frm, frm).wait_recv()

    right, left = lax.rem(z + 1, NZ), lax.rem(z + NZ - 1, NZ)

    def chunk(zz, lo, n):
        return unit.at[pl.ds(lo, n), :, zz, core]

    def to_right(t, zz):
        part = chunk(zz, 0, 4 if t < 3 else 2)
        return copy(part, part, zr_s.at[t], zr_r.at[t], row_of(xy, right, core), col)

    def to_left(t, zz):
        part = chunk(zz, 0 if t < 3 else 2, 4 if t < 3 else 2)
        return copy(part, part, zl_s.at[t], zl_r.at[t], row_of(xy, left, core), col)

    def to_core(o, k):
        part = unit.at[:, :, lax.rem(z + o, NZ), k]
        return copy(part, part, gc_s.at[o], gc_r.at[o], row_of(xy, z, 1 - core), col)

    def at(o):
        return lax.rem(z + NZ + o, NZ)

    to_right(0, z).start()
    to_left(0, z).start()
    to_core(0, core).start()

    def small(i):
        part = pl.ds(pl.multiple_of(i * BLK, BLK), BLK)
        link_b[part, :] = dot(lk_below[part, :], sec_l[...]).astype(BF16)
        link_s[part, :] = dot_cols(lk_beside[part, :], sec_u[...]).astype(BF16)
        base2[part, :] = dot(sec_u[part, :], sec_l[:, own_half])

    each(4, small)
    base1[...] = dot(inv_u[pl.ds(pl.multiple_of(d * 16, 16), 16), :], inv_l[...])

    for t in range(4):
        to_right(t, at(-1 - t)).wait_recv()
        if t < 3:
            to_right(t + 1, at(-1 - t)).start()
            to_core(7 - t, core).start()
        to_left(t, at(1 + t)).wait_recv()
        if t < 3:
            to_left(t + 1, at(1 + t)).start()
            to_core(1 + t, core).start()
    to_core(4, core).start()
    pltpu.make_async_copy(tile, tile, loc_sem.at[0]).wait()
    load_strip.wait()
    for o in range(NZ):
        to_core(o, 1 - core).wait_recv()

    first_block = col * (COLS // BLK)

    def lower_product(blocks, panel):
        def take(k):
            local = blocks[k] - first_block
            inside = jnp.logical_and(local >= 0, local < COLS // BLK)
            block = tile[jnp.clip(local, 0, COLS // BLK - 1)].reshape(ROWS, BLK)
            pick_l[:, pl.ds(pl.multiple_of(k * BLK, BLK), BLK)] = kept(block, inside)

        each(R, take)

        def multiply(i):
            part = pl.ds(pl.multiple_of(i * 256, BLK), 256)
            prod[panel, :, part] = dot(pick_l[...], unit[panel, :, :, :, :, part].reshape(R * BLK, 256))

        each(2, multiply)

    lower_product(list_below, 0)
    lower_product(blocks_below, 1)

    def onto_rows(blocks, panel, at_slot):
        for i in range(3):
            half = row * 3 + i
            block = lax.div(half, 2)
            offset = lax.rem(half, 2)

            place, found = jnp.int32(0), jnp.int32(0)
            for k in range(R):
                hit = (blocks[k] == block).astype(jnp.int32)
                place, found = place + hit * k, found + hit
            place = jnp.minimum(place, R - 1)
            at_xy, at_z = lax.div(place, 2), lax.rem(place, 2) * 4 + offset * 2
            for j in range(2):
                rows = unit[panel, at_xy, at_z + j].reshape(32, W)
                onto[at_slot, pl.ds(64 * i + 32 * j, 32), :] = kept(rows, found)

    onto_rows(list_beside, 2, 0)
    onto_rows(blocks_beside, 3, 1)

    def finish_lower(i):
        part = pl.ds(pl.multiple_of(i * 64, 64), 64)
        first = -prod[0, part, :]
        second = prod[1, part, :]
        first_b = first.astype(BF16)
        third = -second - dot(first_b, link_b[...])
        prod[0, part, :] = first
        prod[1, part, :] = third
        pick_l[part, 0:W] = first_b
        pick_l[part, W : 2 * W] = second.astype(BF16)
        pick_l[part, 2 * W : 3 * W] = third.astype(BF16)

    each(3, finish_lower)

    def sums(i):
        part = pl.ds(pl.multiple_of(i * BLK, BLK), BLK)
        to = pl.ds(i * 8, 8)
        a = onto[0, :, part]
        sums_s[to, 0] = dot_rows(a, pick_l[:, 0:W]).astype(BF16).reshape(8, 16, W)
        sums_s[to, 1] = dot_rows(a, pick_l[:, W : 2 * W]).astype(BF16).reshape(8, 16, W)
        sums_s[to, 2] = dot_rows(onto[1, :, part], pick_l[:, 2 * W : 3 * W]).astype(BF16).reshape(8, 16, W)

    each(4, sums)
    low_s[...] = prod[:, :, other_half].astype(BF16)
    sums_r[d] = sums_s[d]

    def plane_copy(src, dst, s, r, peer):
        pq = lax.div(peer, 2)
        return copy(src, dst, s, r, row_of(lax.div(pq, NK), z, lax.rem(pq, NK)), lax.rem(peer, 2))

    def sums_out(i):
        peer = lax.rem(d + 1 + i, ND)
        return plane_copy(sums_s.at[peer], sums_r.at[d], sm_s.at[i], sm_r.at[i], peer)

    def sums_in(i):
        peer = lax.rem(d + ND - 1 - i, ND)
        return plane_copy(sums_s.at[d], sums_r.at[peer], sm_s.at[i], sm_r.at[i], peer)

    each(ND - 1, lambda i: sums_out(i).start())
    low_out = copy(low_s, low_r, lw_s.at[0], lw_r.at[0], row, 1 - col)
    low_out.start()

    each(NQ - 1, lambda i: aa_copy(i, lax.rem(q + NQ - 1 - i, NQ), q).wait_recv())

    def upper_product(blocks, panel, slot):
        def take(k):
            b = blocks[k]
            inside = lax.rem(lax.div(b, 3), NZ) == z
            first = lax.div(b, 3 * NZ) * 6 + lax.rem(b, 3) * 2
            pick_u[2 * k] = kept(strip[first], inside)
            pick_u[2 * k + 1] = kept(strip[first + 1], inside)

        each(R, take)

        def multiply(i):
            part = pl.ds(pl.multiple_of(i * BLK, BLK), BLK)
            up_s[slot, part, :] = dot_rows(pick_u[:, :, part].reshape(R * BLK, BLK), unit[panel].reshape(R * BLK, W)).astype(BF16)

        each(STRIP // BLK, multiply)

    upper_product(list_beside, 2, 0)
    upper_product(blocks_beside, 3, 1)

    def up_target(t):
        return row_of(xy, core * 4 + lax.div(t, 2), lax.rem(t, 2))

    def up_rows(t):
        return up_s.at[:, pl.ds(pl.multiple_of(t * OWN, 32), OWN), :]

    def up_out(t):
        return copy(up_rows(t), up_r.at[z], up_ss.at[t], up_rs.at[z], up_target(t), col)

    def up_start(t):
        @pl.when(up_target(t) != row)
        def _():
            up_out(t).start()

    feeder = lax.div(z, 4)
    keeps = core == feeder

    @pl.when(keeps)
    def _():
        t_own = (z - core * 4) * 2 + core
        up_r[z] = up_s[:, pl.ds(pl.multiple_of(t_own * OWN, 32), OWN), :]

    each(4, lambda t: up_start(t))

    each(ND - 1, lambda i: sums_in(i).wait_recv())
    total = jnp.zeros((3, 16, W), F32)
    total = lax.fori_loop(0, ND, lambda i, t: t + sums_r[i].astype(F32), total)
    zsum[z] = total.astype(BF16)

    def z_out(i):
        return copy(zsum.at[z], zsum.at[z], zs_s.at[i], zs_r.at[i], row_of(xy, lax.rem(z + 1 + i, NZ), core), col)

    def z_in(i):
        frm = lax.rem(z + NZ - 1 - i, NZ)
        return copy(zsum.at[frm], zsum.at[frm], zs_s.at[i], zs_r.at[i], row_of(xy, frm, core), col)

    each(NZ - 1, lambda i: z_out(i).start())
    each(4, lambda t: up_start(t + 4))

    copy(low_s, low_r, lw_s.at[0], lw_r.at[0], row, 1 - col).wait_recv()
    o_lower[...] = (prod[0, :, own_half] + low_r[0].astype(F32)).astype(BF16)
    o_nlower[...] = (prod[1, :, own_half] + low_r[1].astype(F32)).astype(BF16)

    each(NZ - 1, lambda i: z_in(i).wait_recv())
    total = jnp.zeros((3, 16, W), F32)
    total = lax.fori_loop(0, NZ, lambda i, t: t + zsum[i].astype(F32), total)
    diag = (base1[...] - total[0]).astype(BF16)
    fin[d, 0] = diag
    fin[d, 1] = (total[1] - dot(diag, link_b[...])).astype(BF16)
    fin[d, 2] = total[2].astype(BF16)

    def fin_out(i):
        peer = lax.rem(d + 1 + i, ND)
        return plane_copy(fin.at[d], fin.at[d], fn_s.at[i], fn_r.at[i], peer)

    def fin_in(i):
        peer = lax.rem(d + ND - 1 - i, ND)
        return plane_copy(fin.at[peer], fin.at[peer], fn_s.at[i], fn_r.at[i], peer)

    each(ND - 1, lambda i: fin_out(i).start())

    def up_wait(i):
        @pl.when(jnp.logical_or(i != z, jnp.logical_not(keeps)))
        def _():
            copy(up_rows(0), up_r.at[i], up_ss.at[0], up_rs.at[i], row_of(xy, i, feeder), col).wait_recv()

    each(NZ, up_wait)

    def up_sum(slot):
        return lax.fori_loop(0, NZ, lambda i, t: t + up_r[i, slot].astype(F32), jnp.zeros((OWN, W), F32))

    upper = (-up_sum(0)).astype(BF16)
    o_upper[...] = upper
    o_nupper[...] = (-(up_sum(1) + dot(upper, link_s[...]))).astype(BF16)

    each(ND - 1, lambda i: fin_in(i).wait_recv())
    o_diag[...] = fin[:, 0, :, own_half].reshape(W, HALF)
    o_link[...] = fin[:, 1].reshape(W, W)
    link_half = fin[:, 1, :, own_half].reshape(W, HALF)

    def last(i):
        part = pl.ds(pl.multiple_of(i * BLK, BLK), BLK)
        held = fin[pl.ds(i * 8, 8), 2, :, own_half].reshape(BLK, HALF).astype(F32)
        o_ndiag[part, :] = (base2[part, :] - held - dot_rows(link_s[:, part], link_half)).astype(BF16)

    each(4, last)

    y_out.wait_send()
    for i in (1, 2, 3):
        x_copy(i, x, x).wait_send()
    each(NQ - 1, lambda i: aa_copy(i, q, lax.rem(q + 1 + i, NQ)).wait_send())
    for t in range(4):
        to_right(t, z).wait_send()
        to_left(t, z).wait_send()
    for o in range(NZ):
        to_core(o, core).wait_send()
    each(ND - 1, lambda i: sums_out(i).wait_send())
    low_out.wait_send()
    each(NZ - 1, lambda i: z_out(i).wait_send())
    each(ND - 1, lambda i: fin_out(i).wait_send())

    def up_sent(t):
        @pl.when(up_target(t) != row)
        def _():
            up_out(t).wait_send()

    each(8, up_sent)


def body(*args):
    vm = pl.BlockSpec(memory_space=pltpu.VMEM)
    sm = pl.BlockSpec(memory_space=pltpu.SMEM)
    (anc, p_below, p_beside, inv_l, inv_u, l_below, l_beside, s_below, s_beside, lk_below, lk_beside,
     sec_l, sec_u, b_below, b_beside) = args
    dma = pltpu.SemaphoreType.DMA
    shapes = [(ROWS, HALF), (OWN, W), (W, HALF), (ROWS, HALF), (OWN, W), (W, W), (W, HALF)]
    return pl.pallas_call(
        kernel,
        out_shape=tuple(jax.ShapeDtypeStruct(s, BF16) for s in shapes),
        in_specs=[pl.BlockSpec(memory_space=pl.ANY)] + [vm] * 10 + [sm] * 4,
        out_specs=tuple([vm] * 7),
        scratch_shapes=[
            pltpu.VMEM((COLS // BLK, 3, 64, BLK), BF16),
            pltpu.VMEM((NQ * 3, 64, STRIP), BF16),
            pltpu.VMEM((4, NXY, NZ, NK, 16, W), BF16),
            pltpu.VMEM((ROWS, R * BLK), BF16),
            pltpu.VMEM((2 * R, 64, STRIP), BF16),
            pltpu.VMEM((2, ROWS, W), BF16),
            pltpu.VMEM((2, ROWS, W), F32),
            pltpu.VMEM((2, ROWS, HALF), BF16),
            pltpu.VMEM((2, ROWS, HALF), BF16),
            pltpu.VMEM((ND, 3, 16, W), BF16),
            pltpu.VMEM((ND, 3, 16, W), BF16),
            pltpu.VMEM((NZ, 3, 16, W), BF16),
            pltpu.VMEM((ND, 3, 16, W), BF16),
            pltpu.VMEM((2, STRIP, W), BF16),
            pltpu.VMEM((NZ, 2, OWN, W), BF16),
            pltpu.VMEM((W, W), BF16),
            pltpu.VMEM((W, W), BF16),
            pltpu.VMEM((16, W), F32),
            pltpu.VMEM((W, HALF), F32),
            dma((2,)),
            dma((1,)), dma((1,)),
            dma((3,)), dma((3,)),
            dma((4,)), dma((4,)), dma((4,)), dma((4,)),
            dma((NZ,)), dma((NZ,)),
            dma((NQ - 1,)), dma((NQ - 1,)),
            dma((1,)), dma((1,)),
            dma((ND - 1,)), dma((ND - 1,)),
            dma((NZ - 1,)), dma((NZ - 1,)),
            dma((ND - 1,)), dma((ND - 1,)),
            dma((8,)), dma((NZ,)),
        ],
        compiler_params=pltpu.CompilerParams(
            collective_id=0, has_side_effects=True, vmem_limit_bytes=60 * 1024 * 1024
        ),
    )(anc.reshape(3, 64, COLS), p_below, p_beside, inv_l, inv_u, s_below, s_beside, lk_below, lk_beside, sec_l, sec_u,
      l_below, l_beside, b_below, b_beside)


def solution(mesh):
    panel = P("rows", None)
    return jax.shard_map(
        body,
        mesh=mesh,
        in_specs=(
            P("rows", "cols"), panel, panel, P(), P(), P(), P(), panel, panel,
            P(), P(), P(), P(), P(), P(),
        ),
        out_specs=(
            P("rows", "cols"),
            P(("cols", "rows"), None),
            P(None, "cols"),
            P("rows", "cols"),
            P(("cols", "rows"), None),
            P(),
            P(None, "cols"),
        ),
        check_vma=False,
    )
```

time: 2100 us -> 186 us (0.09)
  waiting for transfers between devices: 1980 us -> 0 us
  Pallas kernels: 0 us -> 174 us
  local copies, waits for them, and re-layouts: 58.1 us -> 11.4 us
  matrix products: 24.1 us -> 0 us
    psum x2 -> x0, waiting for transfers between devices: 1520 us -> none  [the longest x1 1200 us: diag_block(): summed = lax.psum(inner_rows(picked_rows, lower_local), 'rows')]
    all_gather x4 -> x0, waiting for transfers between devices: 423 us -> none  [the longest x1 119 us: body(): lax.all_gather(beside_next, 'rows', axis=0, tiled=True)]
    pallas_call x0 -> x1, Pallas kernels: none -> 174 us  [body(): pl.pallas_call(kernel, out_shape=tuple((jax.ShapeDtypeStruct(s, BF16) for...]
    reduce_scatter x2 -> x0, waiting for transfers between devices: 37.5 us -> none  [lower_block(): lax.psum_scatter(partial_value, 'cols', scatter_dimension=1, tiled=True)]
    dot_general x19 -> x0, matrix products: 24.1 us -> none  [the longest x6 5.74 us: inner_rows(): lax.dot_general(left, right, (((0,), (0,)), ((), ())), preferred_element_...]
    gather x7 -> x0, local copies, waits for them, and re-layouts: 21.1 us -> none  [the longest x3 9.11 us: rows_onto(): picked = jnp.take(panel, position * BLK + offset, axis=0)]
  transfers between devices with their start and end apart: 9 -> 0, of which waited for: 8 -> 0; matrix products, arithmetic and copies ran while one was open for 3% -> 0% of each run, Pallas kernels for 0% -> 0%
where the time goes in v1:
time: 186 us
  Pallas kernels  174 us (94%)
  local copies, waits for them, and re-layouts  11.4 us (6%)
    pallas_call x1, Pallas kernels, body(): pl.pallas_call(kernel, out_shape=tuple((jax.ShapeDtypeStruct(s, BF16) for...  174 us
    unnamed x7, local copies, waits for them, and re-layouts  11.4 us

profile of v1, /device:TPU:153, one launch (start us, length us, event | category | flops | bytes accessed | tf_op | source)
XLA Modules:
  0.0 186.0 jit_solution(11167970998838161759)
XLA Ops:
  0.6 174.0 %shard_map.198 = (bf16[192,256]{1,0:T(8,128)(2,1)}, bf16[96,512]{1,0:T(8,128)(2,1)}, bf16[512,256]{1,0:T(8,128)(2,1)}, bf16[192,256]{1,0:T(8,128)(2,1)}, bf16[96...) custom-call(bf16[3,64,12288]{2,1,0:T(8,128)(2,1)} %bitcast.1, bf16[16,512]{1,0:T(8,128)(2,1)} %p_below.1, ...), custom_call_target="tpu_custom_call" | custom-call | tf_op jit(solution)/shard_map/pallas_call | solution.py:415
  174.7 1.5 copy.29
  176.2 1.5 copy.30
  177.7 1.7 copy.31
  179.4 1.5 copy.32
  181.0 1.5 copy.33
  182.5 1.9 %copy.34 = bf16[512,512]{1,0:T(8,128)(2,1)} copy(bf16[512,512]{1,0:T(8,128)(2,1)} %get-tuple-element.19) | data formatting | bytes 1048576
  184.4 1.7 copy.35

commit v2 on v1

--- a/solution.py
+++ b/solution.py
@@ -51,10 +51,10 @@
     anc, p_below, p_beside, inv_l, inv_u, s_below, s_beside, lk_below, lk_beside, sec_l, sec_u,
     list_below, list_beside, blocks_below, blocks_beside,
     o_lower, o_upper, o_diag, o_nlower, o_nupper, o_link, o_ndiag,
-    tile, strip, unit, pick_l, pick_u, onto, prod, low_s, low_r, sums_s, sums_r, zsum, fin, up_s, up_r,
+    tile, strip, unit, pick_l, pick_u, onto, prod, low_s, low_r, sums_s, half_r, half_s, sums_r, zsum, fin_s, fin, up_s, up_r,
     link_b, link_s, base1, base2,
     loc_sem, gy_s, gy_r, gx_s, gx_r, zr_s, zr_r, zl_s, zl_r, gc_s, gc_r,
-    aa_s, aa_r, lw_s, lw_r, sm_s, sm_r, zs_s, zs_r, fn_s, fn_r, up_ss, up_rs,
+    aa_s, aa_r, lw_s, lw_r, hf_s, hf_r, sm_s, sm_r, zs_s, zs_r, fn_s, fn_r, fc_s, fc_r, up_ss, up_rs,
 ):
     row = lax.axis_index("rows")
     col = lax.axis_index("cols")
@@ -65,6 +65,7 @@
     yh = lax.rem(xy, NY)
     q = xy * NK + core
     d = q * 2 + col
+    e = xy * 2 + col
 
     def row_of(xy_, z_, core_):
         return (xy_ * NZ + z_) * NK + core_
@@ -108,15 +109,17 @@
             device_id_type=MESH,
         )
 
-    def greet_line(i):
-        peer = lax.rem(z + 1 + lax.div(i, NK), NZ)
-        pl.semaphore_signal(
-            barrier, inc=1, device_id=(row_of(xy, peer, lax.rem(i, NK)), col), device_id_type=MESH
-        )
+    def greet(to_row, to_col):
+        pl.semaphore_signal(barrier, inc=1, device_id=(to_row, to_col), device_id_type=MESH)
 
     each(ND - 1, greet_plane)
-    each((NZ - 1) * NK, greet_line)
+    each((NZ - 1) * NK, lambda i: greet(row_of(xy, lax.rem(z + 1 + lax.div(i, NK), NZ), lax.rem(i, NK)), col))
     pl.semaphore_wait(barrier, ND - 1 + (NZ - 1) * NK)
+
+    feeder = lax.div(z, 4)
+
+    def up_target(t):
+        return row_of(xy, core * 4 + lax.div(t, 2), lax.rem(t, 2))
 
     nxy = x * NY + (1 - yh)
     mine = unit.at[:, xy, z, core]
@@ -131,6 +134,14 @@
 
     for i in (1, 3, 2):
         x_copy(i, x, lax.rem(x + i, NX)).start()
+
+    def aa_peer(i, sign):
+        j, a = divmod(i, 4)
+        step = (1, 3, 2, 0)[a]
+        px = lax.rem(x + NX + sign * step, NX)
+        py = lax.rem(yh + (j + a) % 2, NY)
+        pk = lax.rem(core + j // 2, NK)
+        return (px * NY + py) * NK + pk
 
     def aa_copy(i, src_q, to_q):
         return copy(
@@ -140,7 +151,20 @@
             row_of(lax.div(to_q, NK), z, lax.rem(to_q, NK)), col,
         )
 
-    each(NQ - 1, lambda i: aa_copy(i, q, lax.rem(q + 1 + i, NQ)).start())
+    aa_all = [i for i in range(NQ) if ((1, 3, 2, 0)[i % 4], (i // 4 + i % 4) % 2, i // 8) != (0, 0, 0)]
+
+    def aa_out(i):
+        return aa_copy(i, q, aa_peer(i, 1))
+
+    def aa_in(i):
+        return aa_copy(i, aa_peer(i, -1), q)
+
+    def aa_group(j):
+        for i in aa_all:
+            if i // 4 == j:
+                aa_out(i).start()
+
+    aa_group(0)
 
     for i in (1, 3, 2):
         frm = lax.rem(x + NX - i, NX)
@@ -188,6 +212,7 @@
         if t < 3:
             to_left(t + 1, at(1 + t)).start()
             to_core(1 + t, core).start()
+            aa_group(t + 1)
     to_core(4, core).start()
     pltpu.make_async_copy(tile, tile, loc_sem.at[0]).wait()
     load_strip.wait()
@@ -249,33 +274,54 @@
 
     def sums(i):
         part = pl.ds(pl.multiple_of(i * BLK, BLK), BLK)
-        to = pl.ds(i * 8, 8)
+        to = pl.ds(i * 2, 2)
         a = onto[0, :, part]
-        sums_s[to, 0] = dot_rows(a, pick_l[:, 0:W]).astype(BF16).reshape(8, 16, W)
-        sums_s[to, 1] = dot_rows(a, pick_l[:, W : 2 * W]).astype(BF16).reshape(8, 16, W)
-        sums_s[to, 2] = dot_rows(onto[1, :, part], pick_l[:, 2 * W : 3 * W]).astype(BF16).reshape(8, 16, W)
+        sums_s[to, :, :, 0] = dot_rows(a, pick_l[:, 0:W]).astype(BF16).reshape(2, 2, 2, 16, W)
+        sums_s[to, :, :, 1] = dot_rows(a, pick_l[:, W : 2 * W]).astype(BF16).reshape(2, 2, 2, 16, W)
+        sums_s[to, :, :, 2] = dot_rows(onto[1, :, part], pick_l[:, 2 * W : 3 * W]).astype(BF16).reshape(2, 2, 2, 16, W)
 
     each(4, sums)
     low_s[...] = prod[:, :, other_half].astype(BF16)
-    sums_r[d] = sums_s[d]
-
-    def plane_copy(src, dst, s, r, peer):
-        pq = lax.div(peer, 2)
-        return copy(src, dst, s, r, row_of(lax.div(pq, NK), z, lax.rem(pq, NK)), lax.rem(peer, 2))
+
+    half_out = copy(sums_s.at[:, 1 - core], half_r, hf_s.at[0], hf_r.at[0], row_of(xy, z, 1 - core), col)
+    half_out.start()
+    copy(sums_s.at[:, core], half_r, hf_s.at[0], hf_r.at[0], row_of(xy, z, 1 - core), col).wait_recv()
+
+    def halve(i):
+        half_s[i] = (sums_s[i, core].astype(F32) + half_r[i].astype(F32)).astype(BF16)
+
+    each(NXY, halve)
+    sums_r[e] = half_s[xy, col]
+
+    y = yh * 2 + col
+    steps = [
+        (1, 0), (0, 1), (3, 0), (0, 3), (1, 1), (3, 3), (1, 3), (3, 1),
+        (2, 0), (0, 2), (2, 1), (1, 2), (2, 3), (3, 2), (2, 2),
+    ]
+
+    def mate_at(i, sign):
+        px = lax.rem(x + NX + sign * steps[i][0], NX)
+        py = lax.rem(y + 4 + sign * steps[i][1], 4)
+        return px * 4 + py
+
+    def mate(src, dst, s, r, peer):
+        return copy(src, dst, s, r, row_of(lax.div(peer, 2), z, core), lax.rem(peer, 2))
 
     def sums_out(i):
-        peer = lax.rem(d + 1 + i, ND)
-        return plane_copy(sums_s.at[peer], sums_r.at[d], sm_s.at[i], sm_r.at[i], peer)
+        peer = mate_at(i, 1)
+        return mate(half_s.at[lax.div(peer, 2), lax.rem(peer, 2)], sums_r.at[e], sm_s.at[i], sm_r.at[i], peer)
 
     def sums_in(i):
-        peer = lax.rem(d + ND - 1 - i, ND)
-        return plane_copy(sums_s.at[d], sums_r.at[peer], sm_s.at[i], sm_r.at[i], peer)
-
-    each(ND - 1, lambda i: sums_out(i).start())
+        peer = mate_at(i, -1)
+        return mate(half_s.at[xy, col], sums_r.at[peer], sm_s.at[i], sm_r.at[i], peer)
+
+    for i in range(NQ - 1):
+        sums_out(i).start()
     low_out = copy(low_s, low_r, lw_s.at[0], lw_r.at[0], row, 1 - col)
     low_out.start()
 
-    each(NQ - 1, lambda i: aa_copy(i, lax.rem(q + NQ - 1 - i, NQ), q).wait_recv())
+    for i in aa_all:
+        aa_in(i).wait_recv()
 
     def upper_product(blocks, panel, slot):
         def take(k):
@@ -293,74 +339,88 @@
 
         each(STRIP // BLK, multiply)
 
+    def up_out(slot, t):
+        rows = up_s.at[slot, pl.ds(pl.multiple_of(t * OWN, 32), OWN), :]
+        return copy(rows, up_r.at[z, slot], up_ss.at[slot, t], up_rs.at[slot, z], up_target(t), col)
+
+    def up_start(slot):
+        @pl.when(core == feeder)
+        def _():
+            t_own = (z - core * 4) * 2 + core
+            up_r[z, slot] = up_s[slot, pl.ds(pl.multiple_of(t_own * OWN, 32), OWN), :]
+
+        def start(t):
+            @pl.when(up_target(t) != row)
+            def _():
+                up_out(slot, t).start()
+
+        each(NZ, start)
+
     upper_product(list_beside, 2, 0)
+
+    for i in range(NQ - 1):
+        sums_in(i).wait_recv()
+    total = jnp.zeros((3, 16, W), F32)
+    total = lax.fori_loop(0, NQ, lambda i, t: t + sums_r[i].astype(F32), total)
+    zsum[z] = total.astype(BF16)
+
+    z_steps = (1, 7, 2, 6, 3, 5, 4)
+
+    def z_out(i):
+        return copy(zsum.at[z], zsum.at[z], zs_s.at[i], zs_r.at[i], row_of(xy, lax.rem(z + z_steps[i], NZ), core), col)
+
+    def z_in(i):
+        frm = lax.rem(z + NZ - z_steps[i], NZ)
+        return copy(zsum.at[frm], zsum.at[frm], zs_s.at[i], zs_r.at[i], row_of(xy, frm, core), col)
+
+    for i in range(NZ - 1):
+        z_out(i).start()
+    up_start(0)
     upper_product(blocks_beside, 3, 1)
-
-    def up_target(t):
-        return row_of(xy, core * 4 + lax.div(t, 2), lax.rem(t, 2))
-
-    def up_rows(t):
-        return up_s.at[:, pl.ds(pl.multiple_of(t * OWN, 32), OWN), :]
-
-    def up_out(t):
-        return copy(up_rows(t), up_r.at[z], up_ss.at[t], up_rs.at[z], up_target(t), col)
-
-    def up_start(t):
-        @pl.when(up_target(t) != row)
-        def _():
-            up_out(t).start()
-
-    feeder = lax.div(z, 4)
-    keeps = core == feeder
-
-    @pl.when(keeps)
-    def _():
-        t_own = (z - core * 4) * 2 + core
-        up_r[z] = up_s[:, pl.ds(pl.multiple_of(t_own * OWN, 32), OWN), :]
-
-    each(4, lambda t: up_start(t))
-
-    each(ND - 1, lambda i: sums_in(i).wait_recv())
-    total = jnp.zeros((3, 16, W), F32)
-    total = lax.fori_loop(0, ND, lambda i, t: t + sums_r[i].astype(F32), total)
-    zsum[z] = total.astype(BF16)
-
-    def z_out(i):
-        return copy(zsum.at[z], zsum.at[z], zs_s.at[i], zs_r.at[i], row_of(xy, lax.rem(z + 1 + i, NZ), core), col)
-
-    def z_in(i):
-        frm = lax.rem(z + NZ - 1 - i, NZ)
-        return copy(zsum.at[frm], zsum.at[frm], zs_s.at[i], zs_r.at[i], row_of(xy, frm, core), col)
-
-    each(NZ - 1, lambda i: z_out(i).start())
-    each(4, lambda t: up_start(t + 4))
+    up_start(1)
 
     copy(low_s, low_r, lw_s.at[0], lw_r.at[0], row, 1 - col).wait_recv()
     o_lower[...] = (prod[0, :, own_half] + low_r[0].astype(F32)).astype(BF16)
     o_nlower[...] = (prod[1, :, own_half] + low_r[1].astype(F32)).astype(BF16)
 
-    each(NZ - 1, lambda i: z_in(i).wait_recv())
+    for i in range(NZ - 1):
+        z_in(i).wait_recv()
     total = jnp.zeros((3, 16, W), F32)
     total = lax.fori_loop(0, NZ, lambda i, t: t + zsum[i].astype(F32), total)
     diag = (base1[...] - total[0]).astype(BF16)
-    fin[d, 0] = diag
-    fin[d, 1] = (total[1] - dot(diag, link_b[...])).astype(BF16)
-    fin[d, 2] = total[2].astype(BF16)
+    link = (total[1] - dot(diag, link_b[...])).astype(BF16)
+    held = total[2].astype(BF16)
+    for c in range(2):
+        fin_s[c, :, 0:HALF] = diag[:, c * HALF : (c + 1) * HALF]
+        fin_s[c, :, HALF : HALF + W] = link
+        fin_s[c, :, HALF + W :] = held[:, c * HALF : (c + 1) * HALF]
+    fin[xy, core, col] = fin_s[col]
 
     def fin_out(i):
-        peer = lax.rem(d + 1 + i, ND)
-        return plane_copy(fin.at[d], fin.at[d], fn_s.at[i], fn_r.at[i], peer)
+        peer = mate_at(i, 1)
+        return mate(fin_s.at[lax.rem(peer, 2)], fin.at[xy, core, col], fn_s.at[i], fn_r.at[i], peer)
 
     def fin_in(i):
-        peer = lax.rem(d + ND - 1 - i, ND)
-        return plane_copy(fin.at[peer], fin.at[peer], fn_s.at[i], fn_r.at[i], peer)
-
-    each(ND - 1, lambda i: fin_out(i).start())
+        peer = mate_at(i, -1)
+        return mate(fin_s.at[col], fin.at[lax.div(peer, 2), core, lax.rem(peer, 2)], fn_s.at[i], fn_r.at[i], peer)
+
+    def fin_core(k):
+        return copy(fin.at[:, k], fin.at[:, k], fc_s.at[0], fc_r.at[0], row_of(xy, z, 1 - core), col)
+
+    for i in range(NQ - 1):
+        fin_out(i).start()
+    for i in range(NQ - 1):
+        fin_in(i).wait_recv()
+    fin_core(core).start()
 
     def up_wait(i):
-        @pl.when(jnp.logical_or(i != z, jnp.logical_not(keeps)))
+        @pl.when(row_of(xy, i, feeder) != row)
         def _():
-            copy(up_rows(0), up_r.at[i], up_ss.at[0], up_rs.at[i], row_of(xy, i, feeder), col).wait_recv()
+            for slot in range(2):
+                copy(
+                    up_s.at[slot, 0:OWN], up_r.at[i, slot], up_ss.at[slot, 0], up_rs.at[slot, i],
+                    row_of(xy, i, feeder), col,
+                ).wait_recv()
 
     each(NZ, up_wait)
 
@@ -371,14 +431,15 @@
     o_upper[...] = upper
     o_nupper[...] = (-(up_sum(1) + dot(upper, link_s[...]))).astype(BF16)
 
-    each(ND - 1, lambda i: fin_in(i).wait_recv())
-    o_diag[...] = fin[:, 0, :, own_half].reshape(W, HALF)
-    o_link[...] = fin[:, 1].reshape(W, W)
-    link_half = fin[:, 1, :, own_half].reshape(W, HALF)
+    fin_core(1 - core).wait_recv()
+    o_diag[...] = fin[:, :, :, :, 0:HALF].reshape(W, HALF)
+    o_link[...] = fin[:, :, :, :, HALF : HALF + W].reshape(W, W)
+    own_link = pl.ds(pl.multiple_of(HALF + col * HALF, BLK), HALF)
+    link_half = fin[:, :, :, :, own_link].reshape(W, HALF)
 
     def last(i):
         part = pl.ds(pl.multiple_of(i * BLK, BLK), BLK)
-        held = fin[pl.ds(i * 8, 8), 2, :, own_half].reshape(BLK, HALF).astype(F32)
+        held = fin[pl.ds(i * 2, 2), :, :, :, HALF + W :].reshape(BLK, HALF).astype(F32)
         o_ndiag[part, :] = (base2[part, :] - held - dot_rows(link_s[:, part], link_half)).astype(BF16)
 
     each(4, last)
@@ -386,23 +447,34 @@
     y_out.wait_send()
     for i in (1, 2, 3):
         x_copy(i, x, x).wait_send()
-    each(NQ - 1, lambda i: aa_copy(i, q, lax.rem(q + 1 + i, NQ)).wait_send())
+    for i in aa_all:
+        aa_out(i).wait_send()
     for t in range(4):
         to_right(t, z).wait_send()
         to_left(t, z).wait_send()
     for o in range(NZ):
         to_core(o, core).wait_send()
-    each(ND - 1, lambda i: sums_out(i).wait_send())
+    half_out.wait_send()
+    for i in range(NQ - 1):
+        sums_out(i).wait_send()
+        fin_out(i).wait_send()
     low_out.wait_send()
-    each(NZ - 1, lambda i: z_out(i).wait_send())
-    each(ND - 1, lambda i: fin_out(i).wait_send())
+    for i in range(NZ - 1):
+        z_out(i).wait_send()
+    fin_core(core).wait_send()
 
     def up_sent(t):
         @pl.when(up_target(t) != row)
         def _():
-            up_out(t).wait_send()
-
-    each(8, up_sent)
+            up_out(0, t).wait_send()
+            up_out(1, t).wait_send()
+
+    each(NZ, up_sent)
+
+
+def hand_on(*refs):
+    for src, dst in zip(refs[:7], refs[7:]):
+        dst[...] = src[...]
 
 
 def body(*args):
@@ -412,9 +484,10 @@
      sec_l, sec_u, b_below, b_beside) = args
     dma = pltpu.SemaphoreType.DMA
     shapes = [(ROWS, HALF), (OWN, W), (W, HALF), (ROWS, HALF), (OWN, W), (W, W), (W, HALF)]
-    return pl.pallas_call(
+    out_shape = tuple(jax.ShapeDtypeStruct(s, BF16) for s in shapes)
+    made = pl.pallas_call(
         kernel,
-        out_shape=tuple(jax.ShapeDtypeStruct(s, BF16) for s in shapes),
+        out_shape=out_shape,
         in_specs=[pl.BlockSpec(memory_space=pl.ANY)] + [vm] * 10 + [sm] * 4,
         out_specs=tuple([vm] * 7),
         scratch_shapes=[
@@ -427,10 +500,13 @@
             pltpu.VMEM((2, ROWS, W), F32),
             pltpu.VMEM((2, ROWS, HALF), BF16),
             pltpu.VMEM((2, ROWS, HALF), BF16),
-            pltpu.VMEM((ND, 3, 16, W), BF16),
-            pltpu.VMEM((ND, 3, 16, W), BF16),
+            pltpu.VMEM((NXY, NK, 2, 3, 16, W), BF16),
+            pltpu.VMEM((NXY, 2, 3, 16, W), BF16),
+            pltpu.VMEM((NXY, 2, 3, 16, W), BF16),
+            pltpu.VMEM((NQ, 3, 16, W), BF16),
             pltpu.VMEM((NZ, 3, 16, W), BF16),
-            pltpu.VMEM((ND, 3, 16, W), BF16),
+            pltpu.VMEM((2, 16, 2 * W), BF16),
+            pltpu.VMEM((NXY, NK, 2, 16, 2 * W), BF16),
             pltpu.VMEM((2, STRIP, W), BF16),
             pltpu.VMEM((NZ, 2, OWN, W), BF16),
             pltpu.VMEM((W, W), BF16),
@@ -442,18 +518,23 @@
             dma((3,)), dma((3,)),
             dma((4,)), dma((4,)), dma((4,)), dma((4,)),
             dma((NZ,)), dma((NZ,)),
+            dma((NQ,)), dma((NQ,)),
+            dma((1,)), dma((1,)),
+            dma((1,)), dma((1,)),
+            dma((NQ - 1,)), dma((NQ - 1,)),
+            dma((NZ - 1,)), dma((NZ - 1,)),
             dma((NQ - 1,)), dma((NQ - 1,)),
             dma((1,)), dma((1,)),
-            dma((ND - 1,)), dma((ND - 1,)),
-            dma((NZ - 1,)), dma((NZ - 1,)),
-            dma((ND - 1,)), dma((ND - 1,)),
-            dma((8,)), dma((NZ,)),
+            dma((2, NZ)), dma((2, NZ)),
         ],
         compiler_params=pltpu.CompilerParams(
             collective_id=0, has_side_effects=True, vmem_limit_bytes=60 * 1024 * 1024
         ),
     )(anc.reshape(3, 64, COLS), p_below, p_beside, inv_l, inv_u, s_below, s_beside, lk_below, lk_beside, sec_l, sec_u,
       l_below, l_beside, b_below, b_beside)
+    return pl.pallas_call(
+        hand_on, out_shape=out_shape, in_specs=[vm] * 7, out_specs=tuple([vm] * 7)
+    )(*made)
 
 
 def solution(mesh):

time: 186 us -> 137 us (0.74)
  the two profiles are of different devices: /device:TPU:153 before, /device:TPU:73 now
where the time goes in v2:
time: 137 us
  Pallas kernels  136 us (99%)
    pallas_call x1, Pallas kernels, body(): pl.pallas_call(kernel, out_shape=out_shape, in_specs=[pl.BlockSpec(memory...  134 us

profile of v2, /device:TPU:73, one launch (start us, length us, event | category | flops | bytes accessed | tf_op | source)
XLA Modules:
  0.0 136.7 jit_solution(10515268435302691819)
XLA Ops:
  0.6 133.6 %shard_map.198 = (bf16[192,256]{1,0:T(8,128)(2,1)}, bf16[96,512]{1,0:T(8,128)(2,1)}, bf16[512,256]{1,0:T(8,128)(2,1)}, bf16[192,256]{1,0:T(8,128)(2,1)}, bf16[96...) custom-call(bf16[3,64,12288]{2,1,0:T(8,128)(2,1)} %bitcast.1, bf16[16,512]{1,0:T(8,128)(2,1)} %p_below.1, ...), custom_call_target="tpu_custom_call" | custom-call | tf_op jit(solution)/shard_map/pallas_call | solution.py:488
  134.2 2.5 %shard_map.199 = (bf16[192,256]{1,0:T(8,128)(2,1)}, bf16[96,512]{1,0:T(8,128)(2,1)}, bf16[512,256]{1,0:T(8,128)(2,1)}, bf16[192,256]{1,0:T(8,128)(2,1)}, bf16[96...) custom-call(bf16[192,256]{1,0:T(8,128)(2,1)} %get-tuple-element.14.refs_0_, ...), custom_call_target="tpu_custom_call" | custom-call | tf_op jit(solution)/shard_map/pallas_call | solution.py:535
